TPU v7x, 256 devices: a whole 4x4x8 slice. The times are simulated.
256 devices in a mesh: tile: 4 (over y), proj: 16 (over x, z_hi, core), cuts: 4 (over z_lo).
Axes of the slice: x: 4, y: 4, z: 8 (z_hi: 2, z_lo: 4; z = z_hi * 4 + z_lo), core: 2. Of those that a mesh axis runs over, the one named last changes fastest.
Arguments:
- object_field: float32 [64, 2, 384, 2048], P(('proj', 'cuts'), None, None, 'tile'), may hold values from -5 to 5
- probe_field: float32 [2, 256, 256], replicated, may hold values from -6 to 6
- amplitudes: bfloat16 [64, 4, 6, 256, 256], P(('proj', 'cuts'), 'tile'), may hold values from 0 to 16
- pos_rows: int32 [64, 4, 6], P(('proj', 'cuts'), 'tile'), may hold values from 0 to 128
- pos_cols: int32 [64, 4, 6], P(('proj', 'cuts'), 'tile'), may hold values from 0 to 512
- counts: int32 [64, 4], P(('proj', 'cuts'), 'tile'), may hold values from 1 to 6, as said below
- admm_dual: float32 [64, 32, 2048], P(('proj', 'cuts'), None, 'tile'), may hold values from -4 to 4
- volume: float32 [32, 2048, 2048], P('cuts', ('tile', 'proj')), may hold values from -6 to 6
- proj_weights: bfloat16 [16, 2048, 2048], P(None, ('tile', 'proj')), may hold values from -0.125 to 0.125
- ray_weights: float32 [16, 2048], replicated, may hold values from -0.125 to 0.125
- angle_ids: int32 [64], replicated, may hold values from 0 to 15
Outputs:
- new_object: float32 [64, 2, 384, 2048], P(('proj', 'cuts'), None, None, 'tile')
- new_probe: float32 [2, 256, 256], replicated
- new_volume: float32 [32, 2048, 2048], P('cuts', ('tile', 'proj'))
Inputs may be any that keep to these rules, and one draw needn't show every extreme that they name: `counts`: every tile holds at least one live position and at most 6; exactly one tile of one projection holds 6, every other holds at most 3.
All inputs are finite; a program needn't handle non-finite values.
Results may differ from a plain program's by a relative error of at most 0.00095.
The roundings to bfloat16 on the way count: a program that leaves them out, or rounds other values in their place, can miss the bound.
Values may be sent and summed in bfloat16 or wider, within the bound.
A program may use at most 64 MiB of HBM per device.

v0:
```python
import math
import jax
import jax.numpy as jnp
from jax import lax
from jax.sharding import PartitionSpec as P

PB = 256
tomo_step = 1.0


def shifted(value, axis, steps):
    count = lax.axis_size(axis)
    leading, last = (max(0, -steps), min(count, count - steps))
    return lax.ppermute(value, axis, [(source, source + steps) for source in range(leading, last)])


def dft_tables(side):
    indices = jnp.arange(side, dtype=jnp.int32)
    products = indices[:, None] * indices[None, :] % side
    phase_angle = products.astype(jnp.float32) * (2.0 * math.pi / side)
    norm_factor = 1.0 / math.sqrt(side)
    return (
        (jnp.cos(phase_angle) * norm_factor).astype(jnp.bfloat16),
        (-jnp.sin(phase_angle) * norm_factor).astype(jnp.bfloat16),
    )


def matmul(left, right):
    return jnp.dot(left, right, preferred_element_type=jnp.float32)


def complex_matmul(left_real, left_imag, right_real, right_imag):
    out_real = matmul(left_real, right_real) - matmul(left_imag, right_imag)
    out_imag = matmul(left_real, right_imag) + matmul(left_imag, right_real)
    return (out_real, out_imag)


def patch_terms(patch_real, patch_imag, probe_real, probe_imag, amplitude, dft_real, dft_imag):
    wave_real = (probe_real * patch_real - probe_imag * patch_imag).astype(jnp.bfloat16)
    wave_imag = (probe_real * patch_imag + probe_imag * patch_real).astype(jnp.bfloat16)
    half_real, half_imag = complex_matmul(dft_real, dft_imag, wave_real, wave_imag)
    half_real = half_real.astype(jnp.bfloat16)
    half_imag = half_imag.astype(jnp.bfloat16)
    far_real, far_imag = complex_matmul(half_real, half_imag, dft_real, dft_imag)
    modulus = jnp.sqrt(far_real * far_real + far_imag * far_imag + 0.25)
    factor = amplitude.astype(jnp.float32) / modulus - 1.0
    diff_real = (far_real * factor).astype(jnp.bfloat16)
    diff_imag = (far_imag * factor).astype(jnp.bfloat16)
    conj_imag = -dft_imag
    back_half_real, back_half_imag = complex_matmul(dft_real, conj_imag, diff_real, diff_imag)
    back_half_real = back_half_real.astype(jnp.bfloat16)
    back_half_imag = back_half_imag.astype(jnp.bfloat16)
    back_real, back_imag = complex_matmul(back_half_real, back_half_imag, dft_real, conj_imag)
    object_real = probe_real * back_real + probe_imag * back_imag
    object_imag = probe_real * back_imag - probe_imag * back_real
    probe_grad_real = patch_real * back_real + patch_imag * back_imag
    probe_grad_imag = patch_real * back_imag - patch_imag * back_real
    energy = jnp.mean(patch_real * patch_real + patch_imag * patch_imag)
    return (
        jnp.stack([object_real, object_imag]),
        jnp.stack([probe_grad_real, probe_grad_imag]),
        energy,
    )


def tile_edges(values, offset):
    return shifted(values, "tile", offset)


def on_device(
    object_field,
    probe_field,
    amplitudes,
    pos_rows,
    pos_cols,
    counts,
    admm_dual,
    volume,
    proj_weights,
    ray_weights,
    angle_ids,
):
    half_side = PB // 2
    own_object = object_field[0]
    tile_cols = own_object.shape[2]
    from_left = tile_edges(own_object[:, :, tile_cols - half_side :], 1)
    from_right = tile_edges(own_object[:, :, :half_side], -1)
    extended = jnp.concatenate([from_left, own_object, from_right], axis=2)
    dft_real, dft_imag = dft_tables(PB)
    probe_real = probe_field[0]
    probe_imag = probe_field[1]
    zero_index = jnp.zeros((), jnp.int32)
    live_count = counts[0, 0]
    slot_total = amplitudes.shape[2]

    def slot_step(slot_index, state_tuple, weight):
        grad_sum, probe_sum, energy_sum = state_tuple
        anchor = (zero_index, pos_rows[0, 0, slot_index], pos_cols[0, 0, slot_index])
        object_patch = lax.dynamic_slice(extended, anchor, (2, PB, PB))
        object_part, probe_part, energy = patch_terms(
            object_patch[0],
            object_patch[1],
            probe_real,
            probe_imag,
            amplitudes[0, 0, slot_index],
            dft_real,
            dft_imag,
        )
        current = lax.dynamic_slice(grad_sum, anchor, (2, PB, PB))
        grad_sum = lax.dynamic_update_slice(grad_sum, current + weight * object_part, anchor)
        return (grad_sum, probe_sum + weight * probe_part, energy_sum + weight * energy)

    running = (
        jnp.zeros(extended.shape, jnp.float32),
        jnp.zeros((2, PB, PB), jnp.float32),
        jnp.zeros((), jnp.float32),
    )
    running = lax.fori_loop(
        0,
        slot_total,
        lambda slot_index, state_tuple: slot_step(
            slot_index, state_tuple, (slot_index < live_count).astype(jnp.float32)
        ),
        running,
    )
    grad_sum, probe_sum, energy_sum = running
    to_right_edge = tile_edges(grad_sum[:, :, :half_side], -1)
    to_left_edge = tile_edges(grad_sum[:, :, tile_cols + half_side :], 1)
    own_cells = grad_sum[:, :, half_side : half_side + tile_cols]
    own_cells = own_cells.at[:, :, :half_side].add(to_left_edge)
    own_cells = own_cells.at[:, :, tile_cols - half_side :].add(to_right_edge)
    probe_flat = jnp.concatenate([probe_sum.reshape(-1), jnp.broadcast_to(energy_sum, (128,))])
    probe_flat = lax.psum(probe_flat, ("tile", "proj", "cuts"))
    probe_grad = probe_flat[: probe_sum.size].reshape(probe_sum.shape)
    energy = probe_flat[probe_sum.size]
    new_probe = probe_field + probe_grad / (energy + 1e-05)
    probe_peak = jnp.max(probe_real * probe_real + probe_imag * probe_imag)
    new_object = (own_object + own_cells / (probe_peak + 1e-05))[None]
    slab_total = admm_dual.shape[1]
    first_row = (own_object.shape[1] - slab_total) // 2
    slab_values = new_object[:, 1, first_row : first_row + slab_total, :] + admm_dual
    arrived = lax.all_to_all(
        lax.all_to_all(slab_values, "proj", split_axis=2, concat_axis=0, tiled=True),
        "cuts",
        split_axis=1,
        concat_axis=0,
        tiled=True,
    )
    proj_count = lax.axis_size("proj")
    cuts_count = lax.axis_size("cuts")
    slab_dev = arrived.shape[1]
    u_share = arrived.shape[2]
    projections = proj_count * cuts_count
    arrived = arrived.reshape(cuts_count, proj_count, slab_dev, u_share).transpose(1, 0, 2, 3)
    target = (
        arrived.reshape(projections, slab_dev, u_share)
        .transpose(2, 0, 1)
        .reshape(u_share, projections * slab_dev)
    )
    angle_count = ray_weights.shape[0]
    x_share = volume.shape[1]
    width = volume.shape[2]
    onehot = (angle_ids[:, None] == jnp.arange(angle_count, dtype=jnp.int32)[None, :]).astype(
        jnp.float32
    )
    ray_table = jnp.dot(
        onehot, ray_weights, precision=lax.Precision.HIGHEST, preferred_element_type=jnp.float32
    )
    ray_sums = jnp.einsum("zxy,ay->azx", volume, ray_table, precision=lax.Precision.HIGHEST).astype(
        jnp.bfloat16
    )
    spread = onehot.astype(jnp.bfloat16)[:, :, None, None] * ray_sums[:, None, :, :]
    spread = spread.transpose(1, 3, 0, 2).reshape(angle_count * x_share, projections * slab_dev)
    weight_flat = proj_weights.reshape(angle_count * x_share, width)
    partial_term = lax.dot_general(
        weight_flat, spread, (((0,), (0,)), ((), ())), preferred_element_type=jnp.float32
    )
    own_rows = lax.psum_scatter(partial_term, ("tile", "proj"), scatter_dimension=0, tiled=True)
    own_residue = (own_rows - target).astype(jnp.bfloat16)
    residue = lax.all_gather(own_residue, ("tile", "proj"), axis=0, tiled=True)
    backproj = matmul(weight_flat, residue)
    backproj = backproj.reshape(angle_count, x_share, projections, slab_dev)
    back_sums = jnp.einsum("gxaz,ag->azx", backproj, onehot, precision=lax.Precision.HIGHEST)
    gradient = jnp.einsum("azx,ay->zxy", back_sums, ray_table, precision=lax.Precision.HIGHEST)
    new_volume = volume - tomo_step * gradient
    return (new_object, new_probe, new_volume)


def solution(mesh):
    in_specs = (
        P(("proj", "cuts"), None, None, "tile"),
        P(),
        P(("proj", "cuts"), "tile", None, None, None),
        P(("proj", "cuts"), "tile", None),
        P(("proj", "cuts"), "tile", None),
        P(("proj", "cuts"), "tile"),
        P(("proj", "cuts"), None, "tile"),
        P("cuts", ("tile", "proj"), None),
        P(None, ("tile", "proj"), None),
        P(),
        P(),
    )
    out_specs = (P(("proj", "cuts"), None, None, "tile"), P(), P("cuts", ("tile", "proj"), None))
    return jax.shard_map(
        on_device, mesh=mesh, in_specs=in_specs, out_specs=out_specs, check_vma=False
    )
```

profile of v0, /device:TPU:1, one launch (start us, length us, event | category | flops | bytes accessed | tf_op | source)
XLA Modules:
  0.0 628.5 jit_solution(16933225154168796481)
XLA Ops:
  8.1 3.2 copy.17
  13.5 4.0 collective-permute-start
  23.7 3.4 mul.431
  27.1 3.3 convolution_bitcast_fusion
  30.4 5.3 copy.31
  37.5 3.2 pad_maximum_fusion
  42.3 245.5 %while.23 = (s32[]{:T(128)}, f32[2,384,768]{1,2,0:T(8,128)}, f32[2,256,256]{2,1,0:T(8,128)}, f32[]{:T(128)}, s32[1,1,6]{2,1,0:T(1,128)S(1)}, /*index=5*/s32[1,1,...) while((s32[]{:T(128)}, f32[2,384,768]{1,2,0:T(8,128)}, ...), condition=%wide.region_2.3_spmd.clone.clone, body=%wide.region_0.2_spmd.clone.clone.sunk | while | flops 558956544 | bytes 21102956 | solution.py:118
  68.0 3.0 fusion.228
  75.4 6.6 %dynamic_update_slice.13 = f32[2,384,768]{1,2,0:T(8,128)} dynamic-update-slice(f32[2,384,768]{1,2,0:T(8,128)} %get-tuple-element.644, f32[2,256,256]{1,2,0:T(8,128)S(1)} %copy.50, s32[]{:T(128)} %constant.167.clone.1..sunk, s32[]{:T(128)S(6)} %select_n.153, s32[]{:T(128)S(6)} %select_n.154) | dynamic-update-slice | bytes 1048580 | tf_op jit(solution)/shard_map/while/body/eval_jaxpr/dynamic_update_slice | solution.py:110
  116.7 6.0 dynamic_update_slice.13
  157.4 6.2 dynamic_update_slice.13
  198.3 6.3 dynamic_update_slice.13
  239.3 6.6 %dynamic_update_slice.13 = f32[2,384,768]{1,2,0:T(8,128)} dynamic-update-slice(f32[2,384,768]{1,2,0:T(8,128)} %get-tuple-element.644, f32[2,256,256]{1,2,0:T(8,128)S(1)} %copy.50, s32[]{:T(128)} %constant.167.clone.1..sunk, s32[]{:T(128)S(6)} %select_n.153, s32[]{:T(128)S(6)} %select_n.154) | dynamic-update-slice | bytes 1048580 | tf_op jit(solution)/shard_map/while/body/eval_jaxpr/dynamic_update_slice | solution.py:110
  280.6 6.3 %dynamic_update_slice.13 = f32[2,384,768]{1,2,0:T(8,128)} dynamic-update-slice(f32[2,384,768]{1,2,0:T(8,128)} %get-tuple-element.644, f32[2,256,256]{1,2,0:T(8,128)S(1)} %copy.50, s32[]{:T(128)} %constant.167.clone.1..sunk, s32[]{:T(128)S(6)} %select_n.153, s32[]{:T(128)S(6)} %select_n.154) | dynamic-update-slice | bytes 1048580 | tf_op jit(solution)/shard_map/while/body/eval_jaxpr/dynamic_update_slice | solution.py:110
  289.7 5.9 collective-permute-start.2
  303.9 3.2 collective-permute-done.3
  313.5 22.6 %all_to_all.27 = f32[16,1,1024]{2,1,0:T(1,128)S(1)} all-to-all(f32[16,1,1024]{2,1,0:T(1,128)S(1)} %reshape.139), channel_id=1, replica_groups=mesh['tile'=4,'proj'=16,'cuts'=4] {'proj'}, dimensions={0} | all-to-all | bytes 131072 | tf_op jit(solution)/shard_map/all_to_all | solution.py:143
  340.0 3.3 all-to-all-start.1
  344.5 3.3 all-to-all-done.1
  348.8 102.0 %reduce-scatter.4.cloned.1.call-done = f32[32,512]{1,0:T(8,128)} async-done(((f32[2048,512]{1,0:T(8,128)}), f32[32,512]{1,0:T(8,128)}) %reduce-scatter.4.cloned.1.call-update) | async-done | bytes 65552
  452.6 145.6 %all-reduce.3.cloned.1.call-done = f32[131200]{0:T(1024)} async-done(((f32[131200]{0:T(1024)}), f32[131200]{0:T(1024)}) %all-reduce.3.cloned.1.call-update) | async-done | bytes 524816 | tf_op jit(solution)/shard_map/psum | solution.py:133
  604.0 3.0 copy.28
  612.4 3.8 fusion.126
  616.4 4.7 convolution_subtract_fusion.4
  (237 shorter events, 220.2 us)
Async XLA Ops:
  8.0 19.1 %copy-start = (bf16[16,32,2048]{2,1,0:T(8,128)(2,1)S(1)}, bf16[16,32,2048]{2,1,0:T(8,128)(2,1)}, u32[]{:S(2)}) copy-start(bf16[16,32,2048]{2,1,0:T(8,128)(2,1)} %param.25) | copy-start | bytes 6291460
  8.0 10.8 %copy-start.13 = (s32[64]{0:T(128)S(1)}, s32[64]{0:T(128)}, u32[]{:S(2)}) copy-start(s32[64]{0:T(128)} %param.27) | copy-start | bytes 772
  8.0 10.9 %copy-start.9 = (f32[16,2048]{1,0:T(8,128)S(1)}, f32[16,2048]{1,0:T(8,128)}, u32[]{:S(2)}) copy-start(f32[16,2048]{1,0:T(8,128)} %param.26) | copy-start | bytes 393220
  8.0 442.8 %reduce-scatter.4.cloned.1.call-start = ((), (), s32[]{:S(2)}) async-start(), calls=%async_computation.5 | async-start | bytes 4259840
  11.2 8.9 %copy-start.3 = (f32[8,32,2048]{2,1,0:T(8,128)S(1)}, f32[8,32,2048]{2,1,0:T(8,128)}, u32[]{:S(2)}) copy-start(f32[8,32,2048]{2,1,0:T(8,128)} %param.24) | copy-start | bytes 6291460
  13.5 24.0 %collective-permute-start = (f32[2,384,128]{1,2,0:T(8,128)}, f32[2,384,128]{1,2,0:T(8,128)S(1)}, u32[]{:S(2)}, u32[]{:S(2)}) collective-permute-start(f32[2,384,128]{1,2,0:T(8,128)} %get-tuple-element.528), channel_id=1, source_target_pairs={{0,64},{64,128},{128,192},{1,65},{65,129},{129,193},{2,66},{66,130... | collective-permute-start | bytes 1179656 | tf_op jit(solution)/shard_map/ppermute | solution.py:14
  17.6 19.9 %collective-permute-start.1 = (f32[2,384,128]{1,2,0:T(8,128)}, f32[2,384,128]{1,2,0:T(8,128)}, u32[]{:S(2)}, u32[]{:S(2)}) collective-permute-start(f32[2,384,128]{1,2,0:T(8,128)} %get-tuple-element.529), channel_id=1, source_target_pairs={{64,0},{128,64},{192,128},{65,1},{129,65},{193,129},{66,2},{130,66... | collective-permute-start | bytes 1179656 | tf_op jit(solution)/shard_map/ppermute | solution.py:14
  19.4 0.8 copy-start.7
  35.7 1.0 copy-start.5
  40.7 1.6 copy-start.11
  40.7 1.6 copy-start.12
  42.2 254.7 %copy-start.10 = (f32[1,32,512]{2,1,0:T(8,128)S(1)}, f32[1,32,512]{2,1,0:T(8,128)}, u32[]{:S(2)}) copy-start(f32[1,32,512]{2,1,0:T(8,128)} %param.23) | copy-start | bytes 196612
  287.7 9.4 %copy-start.6 = (f32[2,256,256]{2,1,0:T(8,128)S(1)}, f32[2,256,256]{2,1,0:T(8,128)}, u32[]{:S(2)}) copy-start(f32[2,256,256]{2,1,0:T(8,128)} %param.18) | copy-start | bytes 1572868
  289.7 13.1 %collective-permute-start.2 = (f32[2,384,128]{1,2,0:T(8,128)}, f32[2,384,128]{1,2,0:T(8,128)}, u32[]{:S(2)}, u32[]{:S(2)}) collective-permute-start(f32[2,384,128]{1,2,0:T(8,128)} %get-tuple-element.527), channel_id=1, source_target_pairs={{0,64},{64,128},{128,192},{1,65},{65,129},{129,193},{2,66},{66,130... | collective-permute-start | bytes 1179656 | tf_op jit(solution)/shard_map/ppermute | solution.py:14
  295.7 11.4 %collective-permute-start.3 = (f32[2,384,128]{1,2,0:T(8,128)S(1)}, f32[2,384,128]{1,2,0:T(8,128)}, u32[]{:S(2)}, u32[]{:S(2)}) collective-permute-start(f32[2,384,128]{1,2,0:T(8,128)S(1)} %get-tuple-element.526), channel_id=1, source_target_pairs={{64,0},{128,64},{192,128},{65,1},{129,65},{193,129},{66,2},{130,66... | collective-permute-start | bytes 1179656 | tf_op jit(solution)/shard_map/ppermute | solution.py:14
  298.4 9.8 %copy-start.1 = (f32[1,2,384,512]{2,3,1,0:T(8,128)S(1)}, f32[1,2,384,512]{2,3,1,0:T(8,128)}, u32[]{:S(2)}) copy-start(f32[1,2,384,512]{2,3,1,0:T(8,128)} %copy.17) | copy-start | bytes 4718596
  308.4 1.1 copy-start.4
  309.5 33.8 %copy-start.2 = (f32[2,256,256]{2,1,0:T(8,128)S(1)}, f32[2,256,256]{2,1,0:T(8,128)}, u32[]{:S(2)}) copy-start(f32[2,256,256]{2,1,0:T(8,128)} %get-tuple-element.383) | copy-start | bytes 1572868
  340.0 7.9 %all-to-all-start.1 = ((f32[4,1,4096]{2,1,0:T(1,128)}), f32[4,1,4096]{2,1,0:T(1,128)S(1)}, u32[]{:S(2)}, u32[]{:S(2)}) async-start(f32[4,1,4096]{2,1,0:T(1,128)} %reshape.141), calls=%async_computation.1 | async-start | bytes 131072 | tf_op jit(solution)/shard_map/all_to_all | solution.py:142
  343.3 254.9 %all-reduce.3.cloned.1.call-start = ((), (), s32[]{:S(2)}) async-start(), calls=%async_computation.3 | async-start | bytes 1056768 | tf_op jit(solution)/shard_map/psum | solution.py:133
  344.5 262.5 %all-gather.2.cloned.1.call-start = ((), (), s32[]{:S(2)}) async-start(), calls=%async_computation.4 | async-start | bytes 2129920 | tf_op jit(solution)/shard_map/all_gather | solution.py:180
  612.4 4.0 copy-start.8
Sparse Core Ops, SparseCore 0:
  35.8 414.9 reduce-scatter.3
  454.3 86.0 all-gather.1
Sparse Core Ops, SparseCore 1:
  349.8 248.3 all-reduce.2
where the time goes:
time: 632 us; the launch traced here: 629 us
  waiting for transfers between devices  257 us (41%)
  matrix products  143 us (23%)
  local copies, waits for them, and re-layouts  99.8 us (16%)
  other arithmetic  42.6 us (7%)
  loops' own time  30.5 us (5%)
  blocking collectives  22.6 us (4%)
  between operations  17.1 us (3%)
  starting transfers between devices  16 us (3%)
    psum x1, waiting for transfers between devices, on_device(): probe_flat = lax.psum(probe_flat, ('tile', 'proj', 'cuts'))  146 us
    dot_general x97, matrix products, matmul(): return jnp.dot(left, right, preferred_element_type=jnp.float32)  129 us
    unnamed x4, waiting for transfers between devices  102 us
    dynamic_update_slice x12, local copies, waits for them, and re-layouts, slot_step(): lax.dynamic_update_slice(grad_sum, current + weight * object_part, anchor)  39.1 us
    another operation x1, loops' own time, on_device(): lax.fori_loop(0, slot_total, lambda slot_index, state_tuple: slot_step(sl...  30.5 us
    all_to_all x1, blocking collectives, on_device(): lax.all_to_all(slab_values, 'proj', split_axis=2, concat_axis=0, tiled=True)  22.6 us
    unnamed x40, local copies, waits for them, and re-layouts  18.8 us
  transfers between devices with their start and end apart: 8, of which 5 were waited for; matrix products, arithmetic and copies ran while one was open for 42% of the time, Pallas kernels for 0%

commit v1 on v0

--- a/solution.py
+++ b/solution.py
@@ -130,7 +130,8 @@
     own_cells = own_cells.at[:, :, :half_side].add(to_left_edge)
     own_cells = own_cells.at[:, :, tile_cols - half_side :].add(to_right_edge)
     probe_flat = jnp.concatenate([probe_sum.reshape(-1), jnp.broadcast_to(energy_sum, (128,))])
-    probe_flat = lax.psum(probe_flat, ("tile", "proj", "cuts"))
+    one_axis = lax.psum(probe_flat, "tile")
+    probe_flat = lax.psum(one_axis, ("proj", "cuts"))
     probe_grad = probe_flat[: probe_sum.size].reshape(probe_sum.shape)
     energy = probe_flat[probe_sum.size]
     new_probe = probe_field + probe_grad / (energy + 1e-05)

time: 632 us -> 833 us (1.32)
  waiting for transfers between devices: 257 us -> 453 us
    unnamed x4 -> x5, waiting for transfers between devices: 102 us -> 359 us
    psum x1 -> x2, waiting for transfers between devices: 146 us -> 0.02 us  [the longest x1 0.02 us: on_device(): one_axis = lax.psum(probe_flat, 'tile')]
    all_gather x1, waiting for transfers between devices: 0.01 us -> 78.2 us  [on_device(): residue = lax.all_gather(own_residue, ('tile', 'proj'), axis=0, tiled=True)]
    unnamed x40 -> x34, local copies, waits for them, and re-layouts: 18.8 us -> 18 us
  transfers between devices with their start and end apart: 8 -> 9, of which waited for: 5 -> 7; matrix products, arithmetic and copies ran while one was open for 42% -> 5% of each run, Pallas kernels for 0% -> 0%
where the time goes in v1:
time: 833 us; the launch traced here: 829 us
  waiting for transfers between devices  453 us (54%)
  matrix products  145 us (17%)
  local copies, waits for them, and re-layouts  103 us (12%)
  other arithmetic  41.3 us (5%)
  loops' own time  33.2 us (4%)
  blocking collectives  21.8 us (3%)
  between operations  17.2 us (2%)
  starting transfers between devices  15.3 us (2%)
    unnamed x5, waiting for transfers between devices  359 us
    dot_general x97, matrix products, matmul(): return jnp.dot(left, right, preferred_element_type=jnp.float32)  129 us
    all_gather x1, waiting for transfers between devices, on_device(): residue = lax.all_gather(own_residue, ('tile', 'proj'), axis=0, tiled=True)  78.2 us
    dynamic_update_slice x12, local copies, waits for them, and re-layouts, slot_step(): lax.dynamic_update_slice(grad_sum, current + weight * object_part, anchor)  39.1 us
    another operation x1, loops' own time, on_device(): lax.fori_loop(0, slot_total, lambda slot_index, state_tuple: slot_step(sl...  33.2 us
    all_to_all x1, blocking collectives, on_device(): lax.all_to_all(slab_values, 'proj', split_axis=2, concat_axis=0, tiled=True)  21.8 us
    unnamed x34, local copies, waits for them, and re-layouts  18 us
  transfers between devices with their start and end apart: 9, of which 7 were waited for; matrix products, arithmetic and copies ran while one was open for 5% of the time, Pallas kernels for 0%

profile of v1, /device:TPU:1, one launch (start us, length us, event | category | flops | bytes accessed | tf_op | source)
XLA Modules:
  0.0 828.9 jit_solution(5902977416737905498)
XLA Ops:
  8.1 3.2 copy.17
  13.3 4.2 collective-permute-start
  20.0 3.4 fusion.122
  25.5 3.8 collective-permute-done.1
  29.3 3.1 pad_maximum_fusion
  34.1 252.8 %while.23 = (s32[]{:T(128)}, f32[2,384,768]{1,2,0:T(8,128)}, f32[2,256,256]{2,1,0:T(8,128)}, f32[]{:T(128)}, s32[1,1,6]{2,1,0:T(1,128)}, /*index=5*/s32[1,1,6]{2...) while((s32[]{:T(128)}, f32[2,384,768]{1,2,0:T(8,128)}, ...), condition=%wide.region_2.3_spmd.clone.clone, body=%wide.region_0.2_spmd.clone.clone.sunk | while | flops 558956544 | bytes 21102956 | solution.py:118
  68.3 6.5 dynamic_update_slice.13
  110.8 6.0 dynamic_update_slice.13
  152.7 6.2 dynamic_update_slice.13
  194.9 6.3 dynamic_update_slice.13
  237.1 6.5 dynamic_update_slice.13
  279.6 6.3 dynamic_update_slice.13
  290.7 3.4 mul.431
  294.1 3.2 convolution_bitcast_fusion
  297.3 5.4 copy.31
  304.7 5.1 collective-permute-start.2
  314.2 5.9 collective-permute-done.2
  327.3 21.8 %all_to_all.27 = f32[16,1,1024]{2,1,0:T(1,128)S(1)} all-to-all(f32[16,1,1024]{2,1,0:T(1,128)S(1)} %reshape.139), channel_id=1, replica_groups=mesh['tile'=4,'proj'=16,'cuts'=4] {'proj'}, dimensions={0} | all-to-all | bytes 131072 | tf_op jit(solution)/shard_map/all_to_all | solution.py:144
  351.4 3.3 all-to-all-start.1
  355.5 3.8 all-to-all-done.1
  360.3 358.0 %reduce-scatter.4.cloned.1.call-done = f32[32,512]{1,0:T(8,128)} async-done(((f32[2048,512]{1,0:T(8,128)}), f32[32,512]{1,0:T(8,128)}) %reduce-scatter.4.cloned.1.call-update) | async-done | bytes 65552
  728.9 78.2 %all-gather.2.cloned.1.call-done = bf16[2048,512]{1,0:T(8,128)(2,1)} async-done(((bf16[32,512]{1,0:T(8,128)(2,1)}), bf16[2048,512]{1,0:T(8,128)(2,1)}) %all-gather.2.cloned.1.call-update) | async-done | bytes 2097168 | tf_op jit(solution)/shard_map/all_gather | solution.py:181
  812.8 3.8 fusion.126
  816.7 4.7 convolution_subtract_fusion.4
  (234 shorter events, 226.5 us)
Async XLA Ops:
  8.0 286.1 %copy-start = (bf16[16,32,2048]{2,1,0:T(8,128)(2,1)S(1)}, bf16[16,32,2048]{2,1,0:T(8,128)(2,1)}, u32[]{:S(2)}) copy-start(bf16[16,32,2048]{2,1,0:T(8,128)(2,1)} %param.25) | copy-start | bytes 6291460
  8.0 10.8 %copy-start.7 = (f32[16,2048]{1,0:T(8,128)S(1)}, f32[16,2048]{1,0:T(8,128)}, u32[]{:S(2)}) copy-start(f32[16,2048]{1,0:T(8,128)} %param.26) | copy-start | bytes 393220
  8.0 10.8 %copy-start.9 = (s32[64]{0:T(128)S(1)}, s32[64]{0:T(128)}, u32[]{:S(2)}) copy-start(s32[64]{0:T(128)} %param.27) | copy-start | bytes 772
  8.0 346.7 %all-reduce.4.cloned.1.call-start = ((), (), s32[]{:S(2)}) async-start(), calls=%async_computation.3 | async-start | bytes 1056768 | tf_op jit(solution)/shard_map/psum | solution.py:133
  13.3 10.3 %copy-start.3 = (f32[2,256,256]{2,1,0:T(8,128)S(1)}, f32[2,256,256]{2,1,0:T(8,128)}, u32[]{:S(2)}) copy-start(f32[2,256,256]{2,1,0:T(8,128)} %param.18) | copy-start | bytes 1572868
  13.3 12.2 %collective-permute-start = (f32[2,384,128]{1,2,0:T(8,128)}, f32[2,384,128]{1,2,0:T(8,128)S(1)}, u32[]{:S(2)}, u32[]{:S(2)}) collective-permute-start(f32[2,384,128]{1,2,0:T(8,128)} %get-tuple-element.528), channel_id=1, source_target_pairs={{0,64},{64,128},{128,192},{1,65},{65,129},{129,193},{2,66},{66,130... | collective-permute-start | bytes 1179656 | tf_op jit(solution)/shard_map/ppermute | solution.py:14
  17.5 11.9 %collective-permute-start.1 = (f32[2,384,128]{1,2,0:T(8,128)}, f32[2,384,128]{1,2,0:T(8,128)}, u32[]{:S(2)}, u32[]{:S(2)}) collective-permute-start(f32[2,384,128]{1,2,0:T(8,128)} %get-tuple-element.529), channel_id=1, source_target_pairs={{64,0},{128,64},{192,128},{65,1},{129,65},{193,129},{66,2},{130,66... | collective-permute-start | bytes 1179656 | tf_op jit(solution)/shard_map/ppermute | solution.py:14
  19.2 0.8 copy-start.5
  289.1 429.2 %reduce-scatter.4.cloned.1.call-start = ((), (), s32[]{:S(2)}) async-start(), calls=%async_computation.6 | async-start | bytes 4259840
  302.7 8.4 %copy-start.8 = (f32[1,32,512]{2,1,0:T(8,128)S(1)}, f32[1,32,512]{2,1,0:T(8,128)}, u32[]{:S(2)}) copy-start(f32[1,32,512]{2,1,0:T(8,128)} %param.23) | copy-start | bytes 196612
  302.7 8.5 %copy-start.4 = (f32[2,256,256]{2,1,0:T(8,128)S(1)}, f32[2,256,256]{2,1,0:T(8,128)}, u32[]{:S(2)}) copy-start(f32[2,256,256]{2,1,0:T(8,128)} %param.18) | copy-start | bytes 1572868
  304.7 15.4 %collective-permute-start.2 = (f32[2,384,128]{1,2,0:T(8,128)}, f32[2,384,128]{1,2,0:T(8,128)}, u32[]{:S(2)}, u32[]{:S(2)}) collective-permute-start(f32[2,384,128]{1,2,0:T(8,128)} %get-tuple-element.527), channel_id=1, source_target_pairs={{0,64},{64,128},{128,192},{1,65},{65,129},{129,193},{2,66},{66,130... | collective-permute-start | bytes 1179656 | tf_op jit(solution)/shard_map/ppermute | solution.py:14
  309.8 12.8 %collective-permute-start.3 = (f32[2,384,128]{1,2,0:T(8,128)S(1)}, f32[2,384,128]{1,2,0:T(8,128)}, u32[]{:S(2)}, u32[]{:S(2)}) collective-permute-start(f32[2,384,128]{1,2,0:T(8,128)S(1)} %get-tuple-element.526), channel_id=1, source_target_pairs={{64,0},{128,64},{192,128},{65,1},{129,65},{193,129},{66,2},{130,66... | collective-permute-start | bytes 1179656 | tf_op jit(solution)/shard_map/ppermute | solution.py:14
  312.5 11.1 %copy-start.1 = (f32[1,2,384,512]{2,3,1,0:T(8,128)S(1)}, f32[1,2,384,512]{2,3,1,0:T(8,128)}, u32[]{:S(2)}) copy-start(f32[1,2,384,512]{2,3,1,0:T(8,128)} %copy.17) | copy-start | bytes 4718596
  323.8 1.1 copy-start.2
  350.4 369.7 %copy-start.10 = (s32[64]{0:T(128)S(1)}, s32[64]{0:T(128)}, u32[]{:S(2)}) copy-start(s32[64]{0:T(128)} %param.27) | copy-start | bytes 772
  351.4 7.9 all-to-all-start.1
  354.7 368.5 %all-reduce.6.cloned.1.call-start = ((), (), s32[]{:S(2)}) async-start(), calls=%async_computation.4 | async-start | bytes 1056768 | tf_op jit(solution)/shard_map/psum | solution.py:134
  355.4 451.7 %all-gather.2.cloned.1.call-start = ((), (), s32[]{:S(2)}) async-start(), calls=%async_computation.5 | async-start | bytes 2129920 | tf_op jit(solution)/shard_map/all_gather | solution.py:181
  812.8 4.0 copy-start.6
Sparse Core Ops, SparseCore 0:
  289.2 52.1 all-reduce.3
  359.4 178.7 all-reduce.5
Sparse Core Ops, SparseCore 1:
  302.8 415.4 reduce-scatter.3
  721.7 85.4 all-gather.1
